TPU v7x, 32 devices: a whole 2x2x4 slice. The times are simulated.
32 devices in a mesh: gx: 4 (over z), gy: 8 (over y, x, core).
Axes of the slice: x: 2, y: 2, z: 4, core: 2. Of those that a mesh axis runs over, the one named last changes fastest.
Arguments:
- features: bfloat16 [8192, 512], P(('gx', 'gy')), may hold values from -6 to 6
- cotangent: bfloat16 [8192, 512], P(('gx', 'gy')), may hold values from -6 to 6
- self_weight: bfloat16 [3, 512, 512], replicated, may hold values from -0.25 to 0.25
- neigh_weight: bfloat16 [3, 512, 512], replicated, may hold values from -0.25 to 0.25
- block_val: bfloat16 [64, 4, 128, 128], P(('gx', 'gy')), may hold values from -0.25 to 0.25
- block_col: int32 [64, 4], P(('gx', 'gy')), may hold values from 0 to 5
- send_idx: int32 [32, 32, 16], P(('gx', 'gy')), may hold values from 0 to 255
- send_count: int32 [32, 32], P(('gx', 'gy')), may hold values from 0 to 16, as said below
Outputs:
- self_grad: bfloat16 [3, 512, 512], replicated
- neigh_grad: bfloat16 [3, 512, 512], replicated
- input_grad: bfloat16 [8192, 512], P(('gx', 'gy'))
Inputs may be any that keep to these rules, and one draw needn't show every extreme that they name: `send_count`: at most 16 rows from one device to one peer; in every draw some receivers get exactly 16 from every device.
All inputs are finite; a program needn't handle non-finite values.
Results may differ from a plain program's by a relative error of at most 0.02.
Values may be sent and summed in bfloat16 or wider, within the bound.
No kernel may reach another device: no remote copies, remote signals or barrier semaphores. Data moves between devices by JAX's collectives and lax.ppermute only.
A program may use at most 128 MiB of HBM per device.

v0:
```python
import math
import jax
import jax.numpy as jnp
from jax import lax
from jax.sharding import PartitionSpec as P


def gather_sum(extended, values, columns, tile):
    width = extended.shape[1]
    tiled = extended.reshape(-1, tile, width)[columns]
    total = jnp.einsum("rbij,rbjd->rid", values, tiled, preferred_element_type=jnp.float32)
    return total.reshape(-1, width)


def spread_back(upstream, values, columns, ext_tiles, tile):
    width = upstream.shape[1]
    contrib = jnp.einsum(
        "rbij,rid->rbjd",
        values,
        upstream.reshape(-1, tile, width),
        preferred_element_type=jnp.float32,
    )
    onehot = (
        columns.reshape(-1)[None, :] == jnp.arange(ext_tiles, dtype=jnp.int32)[:, None]
    ).astype(jnp.float32)
    total = jnp.einsum(
        "cn,njd->cjd", onehot, contrib.reshape(-1, tile, width), precision=lax.Precision.HIGHEST
    )
    return total.reshape(-1, width)


def per_device(
    features, cotangent, self_weight, neigh_weight, block_val, block_col, send_idx, send_count
):
    outer = lax.axis_size("gx")
    inner = lax.axis_size("gy")
    devices = outer * inner
    node_rows, width = features.shape
    tile = block_val.shape[2]
    layers = self_weight.shape[0]
    slots = send_idx.shape[2]
    halo_rows = devices * slots
    ext_tiles = (node_rows + halo_rows) // tile
    scale = 1.0 / math.sqrt(node_rows * devices)
    row_ids = send_idx.reshape(-1)
    live = (jnp.arange(slots, dtype=jnp.int32)[None, :] < send_count.reshape(-1)[:, None]).reshape(
        -1, 1
    )
    hiddens = [features]
    aggregates = []
    preacts = []
    hidden = features
    for layer_at in range(layers):
        picked = jnp.where(live, jnp.take(hidden, row_ids, axis=0), jnp.zeros((), hidden.dtype))
        picked = picked.reshape(outer, inner, slots, width)
        send_arrived = lax.all_to_all(
            lax.all_to_all(picked, "gx", split_axis=0, concat_axis=0, tiled=True),
            "gy",
            split_axis=1,
            concat_axis=1,
            tiled=True,
        )
        extended = jnp.concatenate([hidden, send_arrived.reshape(halo_rows, width)], axis=0)
        aggregate = gather_sum(extended, block_val, block_col, tile).astype(jnp.bfloat16)
        preact = jnp.dot(
            hidden, self_weight[layer_at], preferred_element_type=jnp.float32
        ) + jnp.dot(aggregate, neigh_weight[layer_at], preferred_element_type=jnp.float32)
        aggregates.append(aggregate)
        preacts.append(preact)
        if layer_at < layers - 1:
            hidden = jax.nn.silu(preact).astype(jnp.bfloat16)
            hiddens.append(hidden)
    transposed = (((0,), (0,)), ((), ()))
    against = (((1,), (1,)), ((), ()))
    self_list = [None] * layers
    neigh_list = [None] * layers
    grad = cotangent
    for layer_at in reversed(range(layers)):
        preact = preacts[layer_at]
        sigma = jax.nn.sigmoid(preact)
        delta = (grad.astype(jnp.float32) * sigma * (1.0 + preact * (1.0 - sigma))).astype(
            jnp.bfloat16
        )
        self_term = lax.dot_general(
            hiddens[layer_at], delta, transposed, preferred_element_type=jnp.float32
        )
        neigh_term = lax.dot_general(
            aggregates[layer_at], delta, transposed, preferred_element_type=jnp.float32
        )
        self_sum, neigh_sum = lax.psum((self_term, neigh_term), ("gx", "gy"))
        self_list[layer_at] = (self_sum * scale).astype(jnp.bfloat16)
        neigh_list[layer_at] = (neigh_sum * scale).astype(jnp.bfloat16)
        own_part = lax.dot_general(
            delta, self_weight[layer_at], against, preferred_element_type=jnp.float32
        )
        upstream = lax.dot_general(
            delta, neigh_weight[layer_at], against, preferred_element_type=jnp.float32
        ).astype(jnp.bfloat16)
        ext_grad = spread_back(upstream, block_val, block_col, ext_tiles, tile)
        outgoing = ext_grad[node_rows:].astype(jnp.bfloat16).reshape(outer, inner, slots, width)
        arrived = lax.all_to_all(
            lax.all_to_all(outgoing, "gx", split_axis=0, concat_axis=0, tiled=True),
            "gy",
            split_axis=1,
            concat_axis=1,
            tiled=True,
        )
        masked = jnp.where(
            live, arrived.reshape(halo_rows, width).astype(jnp.float32), jnp.zeros((), jnp.float32)
        )
        returned = jnp.zeros((node_rows, width), jnp.float32).at[row_ids].add(masked)
        grad = (own_part + ext_grad[:node_rows] + returned).astype(jnp.bfloat16)
    self_grad = jnp.stack(self_list)
    neigh_grad = jnp.stack(neigh_list)
    return (self_grad, neigh_grad, grad)


def solution(mesh):
    return jax.shard_map(
        per_device,
        mesh=mesh,
        in_specs=(
            P(("gx", "gy"), None),
            P(("gx", "gy"), None),
            P(),
            P(),
            P(("gx", "gy"), None, None, None),
            P(("gx", "gy"), None),
            P(("gx", "gy"), None, None),
            P(("gx", "gy"), None),
        ),
        out_specs=(P(), P(), P(("gx", "gy"), None)),
        check_vma=False,
    )
```

profile of v0, /device:TPU:0, one launch (start us, length us, event | category | flops | bytes accessed | tf_op | source)
XLA Modules:
  0.0 399.9 jit_solution(2928996028955188981)
XLA Ops:
  12.1 20.8 %all_to_all.60 = bf16[4,8,16,512]{3,2,1,0:T(8,128)(2,1)S(1)} all-to-all(bf16[4,8,16,512]{3,2,1,0:T(8,128)(2,1)S(1)} %bitcast.184), channel_id=1, replica_groups=mesh['gx'=4,'gy'=8] {'gx'}, dimensions={0} | all-to-all | bytes 1048576 | tf_op jit(solution)/shard_map/all_to_all | solution.py:57
  33.7 3.7 all-to-all-start.1
  38.7 8.5 %all-to-all-done.1 = bf16[4,8,16,512]{3,2,0,1:T(8,128)(2,1)S(1)} async-done(((bf16[4,8,16,512]{3,2,0,1:T(8,128)(2,1)}), bf16[4,8,16,512]{3,2,0,1:T(8,128)(2,1)S(1)}, u32[]{:S(2)}, u32[]{:S(2)}) %all-to-all-start.1) | async-done | bytes 524320 | tf_op jit(solution)/shard_map/all_to_all | solution.py:56
  54.9 14.9 %all_to_all.61 = bf16[4,8,16,512]{3,2,1,0:T(8,128)(2,1)S(1)} all-to-all(bf16[4,8,16,512]{3,2,1,0:T(8,128)(2,1)S(1)} %bitcast.185), channel_id=1, replica_groups=mesh['gx'=4,'gy'=8] {'gx'}, dimensions={0} | all-to-all | bytes 1048576 | tf_op jit(solution)/shard_map/all_to_all | solution.py:57
  70.7 4.3 %all-to-all-start.3 = ((bf16[4,8,16,512]{3,2,0,1:T(8,128)(2,1)}), bf16[4,8,16,512]{3,2,0,1:T(8,128)(2,1)S(1)}, u32[]{:S(2)}, u32[]{:S(2)}) async-start(bf16[4,8,16,512]{3,2,0,1:T(8,128)(2,1)} %copy.111), calls=%async_computation.3 | async-start | bytes 1048576 | tf_op jit(solution)/shard_map/all_to_all | solution.py:56
  76.1 8.6 %all-to-all-done.3 = bf16[4,8,16,512]{3,2,0,1:T(8,128)(2,1)S(1)} async-done(((bf16[4,8,16,512]{3,2,0,1:T(8,128)(2,1)}), bf16[4,8,16,512]{3,2,0,1:T(8,128)(2,1)S(1)}, u32[]{:S(2)}, u32[]{:S(2)}) %all-to-all-start.3) | async-done | bytes 524320 | tf_op jit(solution)/shard_map/all_to_all | solution.py:56
  92.4 14.9 %all_to_all.62 = bf16[4,8,16,512]{3,2,1,0:T(8,128)(2,1)S(1)} all-to-all(bf16[4,8,16,512]{3,2,1,0:T(8,128)(2,1)S(1)} %bitcast.183), channel_id=1, replica_groups=mesh['gx'=4,'gy'=8] {'gx'}, dimensions={0} | all-to-all | bytes 1048576 | tf_op jit(solution)/shard_map/all_to_all | solution.py:57
  108.2 4.3 %all-to-all-start.5 = ((bf16[4,8,16,512]{3,2,0,1:T(8,128)(2,1)}), bf16[4,8,16,512]{3,2,0,1:T(8,128)(2,1)S(1)}, u32[]{:S(2)}, u32[]{:S(2)}) async-start(bf16[4,8,16,512]{3,2,0,1:T(8,128)(2,1)} %copy.113), calls=%async_computation.5 | async-start | bytes 1048576 | tf_op jit(solution)/shard_map/all_to_all | solution.py:56
  113.7 8.5 %all-to-all-done.5 = bf16[4,8,16,512]{3,2,0,1:T(8,128)(2,1)S(1)} async-done(((bf16[4,8,16,512]{3,2,0,1:T(8,128)(2,1)}), bf16[4,8,16,512]{3,2,0,1:T(8,128)(2,1)S(1)}, u32[]{:S(2)}, u32[]{:S(2)}) %all-to-all-start.5) | async-done | bytes 524320 | tf_op jit(solution)/shard_map/all_to_all | solution.py:56
  133.5 4.1 %all-to-all-start.6 = ((bf16[4,8,16,512]{3,2,1,0:T(8,128)(2,1)}), bf16[4,8,16,512]{3,2,1,0:T(8,128)(2,1)}, u32[]{:S(2)}, u32[]{:S(2)}) async-start(bf16[4,8,16,512]{3,2,1,0:T(8,128)(2,1)} %copy.119), calls=%async_computation.6 | async-start | bytes 1048576 | tf_op jit(solution)/shard_map/all_to_all | solution.py:102
  137.7 12.5 %all-to-all-done.6 = bf16[4,8,16,512]{3,2,1,0:T(8,128)(2,1)} async-done(((bf16[4,8,16,512]{3,2,1,0:T(8,128)(2,1)}), bf16[4,8,16,512]{3,2,1,0:T(8,128)(2,1)}, u32[]{:S(2)}, u32[]{:S(2)}) %all-to-all-start.6) | async-done | bytes 524320 | tf_op jit(solution)/shard_map/all_to_all | solution.py:102
  152.1 4.3 %all-to-all-start.7 = ((bf16[4,8,16,512]{3,2,0,1:T(8,128)(2,1)}), bf16[4,8,16,512]{3,2,0,1:T(8,128)(2,1)}, u32[]{:S(2)}, u32[]{:S(2)}) async-start(bf16[4,8,16,512]{3,2,0,1:T(8,128)(2,1)} %copy.120), calls=%async_computation.7 | async-start | bytes 1048576 | tf_op jit(solution)/shard_map/all_to_all | solution.py:101
  158.1 8.1 %all-to-all-done.7 = bf16[4,8,16,512]{3,2,0,1:T(8,128)(2,1)} async-done(((bf16[4,8,16,512]{3,2,0,1:T(8,128)(2,1)}), bf16[4,8,16,512]{3,2,0,1:T(8,128)(2,1)}, u32[]{:S(2)}, u32[]{:S(2)}) %all-to-all-start.7) | async-done | bytes 524320 | tf_op jit(solution)/shard_map/all_to_all | solution.py:101
  167.5 4.0 scatter_fusion
  179.6 4.1 %all-to-all-start.8 = ((bf16[4,8,16,512]{3,2,1,0:T(8,128)(2,1)}), bf16[4,8,16,512]{3,2,1,0:T(8,128)(2,1)}, u32[]{:S(2)}, u32[]{:S(2)}) async-start(bf16[4,8,16,512]{3,2,1,0:T(8,128)(2,1)} %copy.125), calls=%async_computation.8 | async-start | bytes 1048576 | tf_op jit(solution)/shard_map/all_to_all | solution.py:102
  189.1 7.2 %all-to-all-done.8 = bf16[4,8,16,512]{3,2,1,0:T(8,128)(2,1)} async-done(((bf16[4,8,16,512]{3,2,1,0:T(8,128)(2,1)}), bf16[4,8,16,512]{3,2,1,0:T(8,128)(2,1)}, u32[]{:S(2)}, u32[]{:S(2)}) %all-to-all-start.8) | async-done | bytes 524320 | tf_op jit(solution)/shard_map/all_to_all | solution.py:102
  198.2 4.3 %all-to-all-start.9 = ((bf16[4,8,16,512]{3,2,0,1:T(8,128)(2,1)}), bf16[4,8,16,512]{3,2,0,1:T(8,128)(2,1)S(1)}, u32[]{:S(2)}, u32[]{:S(2)}) async-start(bf16[4,8,16,512]{3,2,0,1:T(8,128)(2,1)} %copy.126), calls=%async_computation.9 | async-start | bytes 1048576 | tf_op jit(solution)/shard_map/all_to_all | solution.py:101
  205.2 7.0 %all-to-all-done.9 = bf16[4,8,16,512]{3,2,0,1:T(8,128)(2,1)S(1)} async-done(((bf16[4,8,16,512]{3,2,0,1:T(8,128)(2,1)}), bf16[4,8,16,512]{3,2,0,1:T(8,128)(2,1)S(1)}, u32[]{:S(2)}, u32[]{:S(2)}) %all-to-all-start.9) | async-done | bytes 524320 | tf_op jit(solution)/shard_map/all_to_all | solution.py:101
  212.5 4.0 %scatter_fusion.1 = f32[256,512]{1,0:T(8,128)S(1)} fusion(f32[256,512]{1,0:T(8,128)S(1)} %convolution_add_fusion.1, s32[512]{0:T(512)S(1)} %bitcast.199, f32[512,512]{1,0:T(8,128)S(1)} %bitcast_select_fusion.1), kind=kCustom, calls=%fused_computation.7 | custom fusion | flops 262144 | bytes 3147776 | tf_op jit(solution)/shard_map/scatter-add | solution.py:111
  226.5 22.2 %all_to_all.63 = bf16[4,8,16,512]{3,2,1,0:T(8,128)(2,1)S(1)} all-to-all(bf16[4,8,16,512]{3,2,1,0:T(8,128)(2,1)S(1)} %copy.136), channel_id=1, replica_groups=mesh['gx'=4,'gy'=8] {'gx'}, dimensions={0} | all-to-all | bytes 1048576 | tf_op jit(solution)/shard_map/all_to_all | solution.py:102
  249.5 3.5 all-to-all-start.11
  254.8 7.9 %all-to-all-done.11 = bf16[4,8,16,512]{3,2,0,1:T(8,128)(2,1)S(1)} async-done(((bf16[4,8,16,512]{3,2,0,1:T(8,128)(2,1)}), bf16[4,8,16,512]{3,2,0,1:T(8,128)(2,1)S(1)}, u32[]{:S(2)}, u32[]{:S(2)}) %all-to-all-start.11) | async-done | bytes 524320 | tf_op jit(solution)/shard_map/all_to_all | solution.py:101
  263.0 3.8 scatter_fusion.2
  267.5 117.8 %all-reduce.3.cloned.1.call-done = (f32[512,512]{0,1:T(8,128)}, f32[512,512]{0,1:T(8,128)}, f32[512,512]{0,1:T(8,128)}, f32[512,512]{0,1:T(8,128)}, f32[512,512]{0,1:T(8,128)}, /*index=5*/f32[512,512]{0,1:T(8,128)}) async-done(((f32[512,512]{0,1:T(8,128)}, f32[512,512]{0,1:T(8,128)}, f32[512,512]{0,1:T(8,128)}, f32[512,512]{0,1:T(8,128)}, f32[512,512]{0,1:T(8,128)}, /*index=5*/f32[512,512]{0,1:T(8,128)}), ...) | async-done | bytes 6291472 | tf_op jit(solution)/shard_map/psum | solution.py:90
  (132 shorter events, 81.8 us)
Async XLA Ops:
  7.2 41.7 %copy-start = (bf16[2,4,128,128]{3,2,1,0:T(8,128)(2,1)S(1)}, bf16[2,4,128,128]{3,2,1,0:T(8,128)(2,1)}, u32[]{:S(2)}) copy-start(bf16[2,4,128,128]{3,2,1,0:T(8,128)(2,1)} %param.14) | copy-start | bytes 786436
  12.1 25.4 %copy-start.17 = (s32[2,4]{1,0:T(2,128)S(1)}, s32[2,4]{1,0:T(2,128)}, u32[]{:S(2)}) copy-start(s32[2,4]{1,0:T(2,128)} %param.15) | copy-start | bytes 100
  12.1 25.5 %copy-start.1 = (bf16[256,512]{1,0:T(8,128)(2,1)S(1)}, bf16[256,512]{1,0:T(8,128)(2,1)}, u32[]{:S(2)}) copy-start(bf16[256,512]{1,0:T(8,128)(2,1)} %param.10) | copy-start | bytes 786436
  12.1 25.4 %copy-start.2 = (bf16[3,512,512]{2,1,0:T(8,128)(2,1)S(1)}, bf16[3,512,512]{2,1,0:T(8,128)(2,1)}, u32[]{:S(2)}) copy-start(bf16[3,512,512]{2,1,0:T(8,128)(2,1)} %param.12) | copy-start | bytes 4718596
  33.7 13.4 %all-to-all-start.1 = ((bf16[4,8,16,512]{3,2,0,1:T(8,128)(2,1)}), bf16[4,8,16,512]{3,2,0,1:T(8,128)(2,1)S(1)}, u32[]{:S(2)}, u32[]{:S(2)}) async-start(bf16[4,8,16,512]{3,2,0,1:T(8,128)(2,1)} %copy.109), calls=%async_computation.1 | async-start | bytes 1048576 | tf_op jit(solution)/shard_map/all_to_all | solution.py:56
  50.5 2.3 copy-start.7
  70.7 14.0 %all-to-all-start.3 = ((bf16[4,8,16,512]{3,2,0,1:T(8,128)(2,1)}), bf16[4,8,16,512]{3,2,0,1:T(8,128)(2,1)S(1)}, u32[]{:S(2)}, u32[]{:S(2)}) async-start(bf16[4,8,16,512]{3,2,0,1:T(8,128)(2,1)} %copy.111), calls=%async_computation.3 | async-start | bytes 1048576 | tf_op jit(solution)/shard_map/all_to_all | solution.py:56
  88.0 2.3 copy-start.9
  108.2 14.0 %all-to-all-start.5 = ((bf16[4,8,16,512]{3,2,0,1:T(8,128)(2,1)}), bf16[4,8,16,512]{3,2,0,1:T(8,128)(2,1)S(1)}, u32[]{:S(2)}, u32[]{:S(2)}) async-start(bf16[4,8,16,512]{3,2,0,1:T(8,128)(2,1)} %copy.113), calls=%async_computation.5 | async-start | bytes 1048576 | tf_op jit(solution)/shard_map/all_to_all | solution.py:56
  123.3 2.3 copy-start.11
  125.6 31.2 %copy-start.3 = (bf16[256,512]{1,0:T(8,128)(2,1)}, bf16[256,512]{1,0:T(8,128)(2,1)S(1)}, u32[]{:S(2)}) copy-start(bf16[256,512]{1,0:T(8,128)(2,1)S(1)} %multiply_convert_fusion.8) | copy-start | bytes 786436
  133.5 16.7 %all-to-all-start.6 = ((bf16[4,8,16,512]{3,2,1,0:T(8,128)(2,1)}), bf16[4,8,16,512]{3,2,1,0:T(8,128)(2,1)}, u32[]{:S(2)}, u32[]{:S(2)}) async-start(bf16[4,8,16,512]{3,2,1,0:T(8,128)(2,1)} %copy.119), calls=%async_computation.6 | async-start | bytes 1048576 | tf_op jit(solution)/shard_map/all_to_all | solution.py:102
  152.1 14.1 %all-to-all-start.7 = ((bf16[4,8,16,512]{3,2,0,1:T(8,128)(2,1)}), bf16[4,8,16,512]{3,2,0,1:T(8,128)(2,1)}, u32[]{:S(2)}, u32[]{:S(2)}) async-start(bf16[4,8,16,512]{3,2,0,1:T(8,128)(2,1)} %copy.120), calls=%async_computation.7 | async-start | bytes 1048576 | tf_op jit(solution)/shard_map/all_to_all | solution.py:101
  167.5 4.0 %copy-start.13 = (f32[256,512]{1,0:T(8,128)S(1)}, f32[256,512]{1,0:T(8,128)}, u32[]{:S(2)}) copy-start(f32[256,512]{1,0:T(8,128)} %get-tuple-element.28) | copy-start | bytes 1572868
  179.6 16.7 %all-to-all-start.8 = ((bf16[4,8,16,512]{3,2,1,0:T(8,128)(2,1)}), bf16[4,8,16,512]{3,2,1,0:T(8,128)(2,1)}, u32[]{:S(2)}, u32[]{:S(2)}) async-start(bf16[4,8,16,512]{3,2,1,0:T(8,128)(2,1)} %copy.125), calls=%async_computation.8 | async-start | bytes 1048576 | tf_op jit(solution)/shard_map/all_to_all | solution.py:102
  183.7 2.4 copy-start.4
  186.1 1.7 copy-start.10
  198.2 14.0 %all-to-all-start.9 = ((bf16[4,8,16,512]{3,2,0,1:T(8,128)(2,1)}), bf16[4,8,16,512]{3,2,0,1:T(8,128)(2,1)S(1)}, u32[]{:S(2)}, u32[]{:S(2)}) async-start(bf16[4,8,16,512]{3,2,0,1:T(8,128)(2,1)} %copy.126), calls=%async_computation.9 | async-start | bytes 1048576 | tf_op jit(solution)/shard_map/all_to_all | solution.py:101
  202.5 182.8 %all-reduce.3.cloned.1.call-start = ((), (), s32[]{:S(2)}) async-start(), calls=%async_computation.12 | async-start | bytes 12582912 | tf_op jit(solution)/shard_map/psum | solution.py:90
  212.5 4.1 %copy-start.12 = (f32[256,512]{1,0:T(8,128)S(1)}, f32[256,512]{1,0:T(8,128)}, u32[]{:S(2)}) copy-start(f32[256,512]{1,0:T(8,128)} %get-tuple-element.26) | copy-start | bytes 1572868
  212.5 4.3 %copy-start.8 = (bf16[2,512,128]{1,2,0:T(8,128)(2,1)S(1)}, bf16[2,512,128]{1,2,0:T(8,128)(2,1)}, u32[]{:S(2)}) copy-start(bf16[2,512,128]{1,2,0:T(8,128)(2,1)} %copy-done.7) | copy-start | bytes 786436
  249.5 13.1 %all-to-all-start.11 = ((bf16[4,8,16,512]{3,2,0,1:T(8,128)(2,1)}), bf16[4,8,16,512]{3,2,0,1:T(8,128)(2,1)S(1)}, u32[]{:S(2)}, u32[]{:S(2)}) async-start(bf16[4,8,16,512]{3,2,0,1:T(8,128)(2,1)} %copy.137), calls=%async_computation.11 | async-start | bytes 1048576 | tf_op jit(solution)/shard_map/all_to_all | solution.py:101
  385.3 2.0 copy-start.5
  385.3 2.2 copy-start.6
  (4 other events, 5.4 us)
Sparse Core Ops, SparseCore 0:
  219.6 165.6 all-reduce.2
where the time goes:
time: 402 us; the launch traced here: 400 us
  waiting for transfers between devices  186 us (46%)
  blocking collectives  72.8 us (18%)
  matrix products  39.5 us (10%)
  local copies, waits for them, and re-layouts  34.6 us (9%)
  starting transfers between devices  32.8 us (8%)
  other arithmetic  19.4 us (5%)
  between operations  14.7 us (4%)
    psum x1, waiting for transfers between devices, per_device(): self_sum, neigh_sum = lax.psum((self_term, neigh_term), ('gx', 'gy'))  118 us
    all_to_all x3, blocking collectives, per_device(): lax.all_to_all(picked, 'gx', split_axis=0, concat_axis=0, tiled=True)  50.6 us
    all_to_all x3, waiting for transfers between devices, per_device(): lax.all_to_all(lax.all_to_all(picked, 'gx', split_axis=0, concat_axis=0,...  25.7 us
    all_to_all x3, waiting for transfers between devices, per_device(): lax.all_to_all(lax.all_to_all(outgoing, 'gx', split_axis=0, concat_axis=0...  23 us
    all_to_all x1, blocking collectives, per_device(): lax.all_to_all(outgoing, 'gx', split_axis=0, concat_axis=0, tiled=True)  22.2 us
    all_to_all x2, waiting for transfers between devices, per_device(): lax.all_to_all(outgoing, 'gx', split_axis=0, concat_axis=0, tiled=True)  19.7 us
    all_to_all x3, starting transfers between devices, per_device(): lax.all_to_all(lax.all_to_all(picked, 'gx', split_axis=0, concat_axis=0,...  12.4 us
    all_to_all x3, starting transfers between devices, per_device(): lax.all_to_all(lax.all_to_all(outgoing, 'gx', split_axis=0, concat_axis=0...  12.1 us
  transfers between devices with their start and end apart: 9, of which 9 were waited for; matrix products, arithmetic and copies ran while one was open for 7% of the time, Pallas kernels for 0%

commit v1 on v0

--- a/solution.py
+++ b/solution.py
@@ -98,12 +98,10 @@
         ).astype(jnp.bfloat16)
         ext_grad = spread_back(upstream, block_val, block_col, ext_tiles, tile)
         outgoing = ext_grad[node_rows:].astype(jnp.bfloat16).reshape(outer, inner, slots, width)
-        arrived = lax.all_to_all(
-            lax.all_to_all(outgoing, "gx", split_axis=0, concat_axis=0, tiled=True),
-            "gy",
-            split_axis=1,
-            concat_axis=1,
-            tiled=True,
+        local_x = lax.all_to_all(outgoing, "gx", split_axis=0, concat_axis=0, tiled=True)
+        arrived = jnp.concatenate(
+            lax.all_to_all(jnp.stack(jnp.split(local_x, lax.axis_size("gy"), axis=1)), "gy", 0, 0),
+            axis=1,
         )
         masked = jnp.where(
             live, arrived.reshape(halo_rows, width).astype(jnp.float32), jnp.zeros((), jnp.float32)

time: 402 us -> 430 us (1.070)
  local copies, waits for them, and re-layouts: 34.6 us -> 59.5 us
  blocking collectives: 72.8 us -> 50.6 us
  waiting for transfers between devices: 186 us -> 206 us
  starting transfers between devices: 32.8 us -> 37.1 us
    unnamed x41 -> x66, local copies, waits for them, and re-layouts: 4.99 us -> 31.2 us
    all_to_all x1 -> x0, blocking collectives: 22.2 us -> none  [per_device(): lax.all_to_all(outgoing, 'gx', split_axis=0, concat_axis=0, tiled=True)]
    all_to_all x2 -> x3, waiting for transfers between devices: 19.7 us -> 28.5 us  [per_device(): lax.all_to_all(outgoing, 'gx', split_axis=0, concat_axis=0, tiled=True)]
    psum x1, waiting for transfers between devices: 118 us -> 125 us  [per_device(): self_sum, neigh_sum = lax.psum((self_term, neigh_term), ('gx', 'gy'))]
    all_to_all x3 -> x0, local copies, waits for them, and re-layouts: 4.59 us -> none  [per_device(): lax.all_to_all(outgoing, 'gx', split_axis=0, concat_axis=0, tiled=True)]
    all_to_all x2 -> x3, starting transfers between devices: 8.28 us -> 11.7 us  [per_device(): lax.all_to_all(outgoing, 'gx', split_axis=0, concat_axis=0, tiled=True)]
  transfers between devices with their start and end apart: 9 -> 10, of which waited for: 9 -> 10; matrix products, arithmetic and copies ran while one was open for 7% -> 7% of each run, Pallas kernels for 0% -> 0%
where the time goes in v1:
time: 430 us; the launch traced here: 428 us
  waiting for transfers between devices  206 us (48%)
  local copies, waits for them, and re-layouts  59.5 us (14%)
  blocking collectives  50.6 us (12%)
  matrix products  40.5 us (9%)
  starting transfers between devices  37.1 us (9%)
  other arithmetic  19.5 us (5%)
  between operations  14.7 us (3%)
    psum x1, waiting for transfers between devices, per_device(): self_sum, neigh_sum = lax.psum((self_term, neigh_term), ('gx', 'gy'))  125 us
    all_to_all x3, blocking collectives, per_device(): lax.all_to_all(picked, 'gx', split_axis=0, concat_axis=0, tiled=True)  50.6 us
    unnamed x66, local copies, waits for them, and re-layouts  31.2 us
    all_to_all x3, waiting for transfers between devices, per_device(): lax.all_to_all(outgoing, 'gx', split_axis=0, concat_axis=0, tiled=True)  28.5 us
    all_to_all x3, waiting for transfers between devices, per_device(): lax.all_to_all(jnp.stack(jnp.split(local_x, lax.axis_size('gy'), axis=1))...  26.7 us
    all_to_all x3, waiting for transfers between devices, per_device(): lax.all_to_all(lax.all_to_all(picked, 'gx', split_axis=0, concat_axis=0,...  25.7 us
    all_to_all x3, starting transfers between devices, per_device(): lax.all_to_all(jnp.stack(jnp.split(local_x, lax.axis_size('gy'), axis=1))...  13 us
    all_to_all x3, starting transfers between devices, per_device(): lax.all_to_all(lax.all_to_all(picked, 'gx', split_axis=0, concat_axis=0,...  12.4 us
  transfers between devices with their start and end apart: 10, of which 10 were waited for; matrix products, arithmetic and copies ran while one was open for 7% of the time, Pallas kernels for 0%

profile of v1, /device:TPU:0, one launch (start us, length us, event | category | flops | bytes accessed | tf_op | source)
XLA Modules:
  0.0 427.7 jit_solution(13328187796087341361)
XLA Ops:
  12.9 20.8 %all_to_all.60 = bf16[4,8,16,512]{3,2,1,0:T(8,128)(2,1)S(1)} all-to-all(bf16[4,8,16,512]{3,2,1,0:T(8,128)(2,1)S(1)} %bitcast.328), channel_id=1, replica_groups=mesh['gx'=4,'gy'=8] {'gx'}, dimensions={0} | all-to-all | bytes 1048576 | tf_op jit(solution)/shard_map/all_to_all | solution.py:57
  34.5 3.7 all-to-all-start.1
  39.3 8.6 %all-to-all-done.1 = bf16[4,8,16,512]{3,2,0,1:T(8,128)(2,1)S(1)} async-done(((bf16[4,8,16,512]{3,2,0,1:T(8,128)(2,1)}), bf16[4,8,16,512]{3,2,0,1:T(8,128)(2,1)S(1)}, u32[]{:S(2)}, u32[]{:S(2)}) %all-to-all-start.1) | async-done | bytes 524320 | tf_op jit(solution)/shard_map/all_to_all | solution.py:56
  55.7 14.9 %all_to_all.61 = bf16[4,8,16,512]{3,2,1,0:T(8,128)(2,1)S(1)} all-to-all(bf16[4,8,16,512]{3,2,1,0:T(8,128)(2,1)S(1)} %bitcast.329), channel_id=1, replica_groups=mesh['gx'=4,'gy'=8] {'gx'}, dimensions={0} | all-to-all | bytes 1048576 | tf_op jit(solution)/shard_map/all_to_all | solution.py:57
  71.4 4.3 %all-to-all-start.3 = ((bf16[4,8,16,512]{3,2,0,1:T(8,128)(2,1)}), bf16[4,8,16,512]{3,2,0,1:T(8,128)(2,1)S(1)}, u32[]{:S(2)}, u32[]{:S(2)}) async-start(bf16[4,8,16,512]{3,2,0,1:T(8,128)(2,1)} %copy.195), calls=%async_computation.3 | async-start | bytes 1048576 | tf_op jit(solution)/shard_map/all_to_all | solution.py:56
  76.9 8.6 %all-to-all-done.3 = bf16[4,8,16,512]{3,2,0,1:T(8,128)(2,1)S(1)} async-done(((bf16[4,8,16,512]{3,2,0,1:T(8,128)(2,1)}), bf16[4,8,16,512]{3,2,0,1:T(8,128)(2,1)S(1)}, u32[]{:S(2)}, u32[]{:S(2)}) %all-to-all-start.3) | async-done | bytes 524320 | tf_op jit(solution)/shard_map/all_to_all | solution.py:56
  93.2 14.9 %all_to_all.62 = bf16[4,8,16,512]{3,2,1,0:T(8,128)(2,1)S(1)} all-to-all(bf16[4,8,16,512]{3,2,1,0:T(8,128)(2,1)S(1)} %bitcast.327), channel_id=1, replica_groups=mesh['gx'=4,'gy'=8] {'gx'}, dimensions={0} | all-to-all | bytes 1048576 | tf_op jit(solution)/shard_map/all_to_all | solution.py:57
  109.0 4.3 %all-to-all-start.5 = ((bf16[4,8,16,512]{3,2,0,1:T(8,128)(2,1)}), bf16[4,8,16,512]{3,2,0,1:T(8,128)(2,1)S(1)}, u32[]{:S(2)}, u32[]{:S(2)}) async-start(bf16[4,8,16,512]{3,2,0,1:T(8,128)(2,1)} %copy.197), calls=%async_computation.5 | async-start | bytes 1048576 | tf_op jit(solution)/shard_map/all_to_all | solution.py:56
  114.4 8.5 %all-to-all-done.5 = bf16[4,8,16,512]{3,2,0,1:T(8,128)(2,1)S(1)} async-done(((bf16[4,8,16,512]{3,2,0,1:T(8,128)(2,1)}), bf16[4,8,16,512]{3,2,0,1:T(8,128)(2,1)S(1)}, u32[]{:S(2)}, u32[]{:S(2)}) %all-to-all-start.5) | async-done | bytes 524320 | tf_op jit(solution)/shard_map/all_to_all | solution.py:56
  134.2 4.1 all-to-all-start.6
  138.4 12.5 %all-to-all-done.6 = bf16[4,8,16,512]{3,2,1,0:T(8,128)(2,1)} async-done(((bf16[4,8,16,512]{3,2,1,0:T(8,128)(2,1)}), bf16[4,8,16,512]{3,2,1,0:T(8,128)(2,1)}, u32[]{:S(2)}, u32[]{:S(2)}) %all-to-all-start.6) | async-done | bytes 524320 | tf_op jit(solution)/shard_map/all_to_all | solution.py:101
  162.7 4.3 %all-to-all-start.7 = ((bf16[8,4,1,16,512]{4,3,1,2,0:T(8,128)(2,1)}), bf16[8,4,1,16,512]{4,3,1,2,0:T(8,128)(2,1)}, u32[]{:S(2)}, u32[]{:S(2)}) async-start(bf16[8,4,1,16,512]{4,3,1,2,0:T(8,128)(2,1)} %fusion.54), calls=%async_computation.7 | async-start | bytes 1048576 | tf_op jit(solution)/shard_map/all_to_all | solution.py:103
  168.8 8.1 %all-to-all-done.7 = bf16[8,4,1,16,512]{4,3,1,2,0:T(8,128)(2,1)} async-done(((bf16[8,4,1,16,512]{4,3,1,2,0:T(8,128)(2,1)}), bf16[8,4,1,16,512]{4,3,1,2,0:T(8,128)(2,1)}, u32[]{:S(2)}, u32[]{:S(2)}) %all-to-all-start.7) | async-done | bytes 524320 | tf_op jit(solution)/shard_map/all_to_all | solution.py:103
  178.3 4.0 scatter_fusion
  190.3 4.1 all-to-all-start.8
  199.9 7.2 %all-to-all-done.8 = bf16[4,8,16,512]{3,2,1,0:T(8,128)(2,1)} async-done(((bf16[4,8,16,512]{3,2,1,0:T(8,128)(2,1)}), bf16[4,8,16,512]{3,2,1,0:T(8,128)(2,1)}, u32[]{:S(2)}, u32[]{:S(2)}) %all-to-all-start.8) | async-done | bytes 524320 | tf_op jit(solution)/shard_map/all_to_all | solution.py:101
  218.7 4.3 %all-to-all-start.9 = ((bf16[8,4,1,16,512]{4,3,1,2,0:T(8,128)(2,1)}), bf16[8,4,1,16,512]{4,3,1,2,0:T(8,128)(2,1)S(1)}, u32[]{:S(2)}, u32[]{:S(2)}) async-start(bf16[8,4,1,16,512]{4,3,1,2,0:T(8,128)(2,1)} %fusion.46), calls=%async_computation.9 | async-start | bytes 1048576 | tf_op jit(solution)/shard_map/all_to_all | solution.py:103
  225.7 7.0 %all-to-all-done.9 = bf16[8,4,1,16,512]{4,3,1,2,0:T(8,128)(2,1)S(1)} async-done(((bf16[8,4,1,16,512]{4,3,1,2,0:T(8,128)(2,1)}), bf16[8,4,1,16,512]{4,3,1,2,0:T(8,128)(2,1)S(1)}, u32[]{:S(2)}, u32[]{:S(2)}) %all-to-all-start.9) | async-done | bytes 524320 | tf_op jit(solution)/shard_map/all_to_all | solution.py:103
  233.1 4.0 scatter_fusion.1
  252.4 8.8 %all-to-all-done.10 = bf16[4,8,16,512]{3,2,1,0:T(8,128)(2,1)S(1)} async-done(((bf16[4,8,16,512]{3,2,1,0:T(8,128)(2,1)}), bf16[4,8,16,512]{3,2,1,0:T(8,128)(2,1)S(1)}, u32[]{:S(2)}, u32[]{:S(2)}) %all-to-all-start.10) | async-done | bytes 524320 | tf_op jit(solution)/shard_map/all_to_all | solution.py:101
  266.1 4.3 %all-to-all-start.11 = ((bf16[8,4,1,16,512]{4,3,1,2,0:T(8,128)(2,1)}), bf16[8,4,1,16,512]{4,3,1,2,0:T(8,128)(2,1)S(1)}, u32[]{:S(2)}, u32[]{:S(2)}) async-start(bf16[8,4,1,16,512]{4,3,1,2,0:T(8,128)(2,1)} %fusion.38), calls=%async_computation.11 | async-start | bytes 1048576 | tf_op jit(solution)/shard_map/all_to_all | solution.py:103
  272.2 11.6 %all-to-all-done.11 = bf16[8,4,1,16,512]{4,3,1,2,0:T(8,128)(2,1)S(1)} async-done(((bf16[8,4,1,16,512]{4,3,1,2,0:T(8,128)(2,1)}), bf16[8,4,1,16,512]{4,3,1,2,0:T(8,128)(2,1)S(1)}, u32[]{:S(2)}, u32[]{:S(2)}) %all-to-all-start.11) | async-done | bytes 524320 | tf_op jit(solution)/shard_map/all_to_all | solution.py:103
  284.2 3.8 scatter_fusion.2
  288.7 125.0 %all-reduce.3.cloned.1.call-done = (f32[512,512]{0,1:T(8,128)}, f32[512,512]{0,1:T(8,128)}, f32[512,512]{0,1:T(8,128)}, f32[512,512]{0,1:T(8,128)}, f32[512,512]{0,1:T(8,128)}, /*index=5*/f32[512,512]{0,1:T(8,128)}) async-done(((f32[512,512]{0,1:T(8,128)}, f32[512,512]{0,1:T(8,128)}, f32[512,512]{0,1:T(8,128)}, f32[512,512]{0,1:T(8,128)}, f32[512,512]{0,1:T(8,128)}, /*index=5*/f32[512,512]{0,1:T(8,128)}), ...) | async-done | bytes 6291472 | tf_op jit(solution)/shard_map/psum | solution.py:90
  (163 shorter events, 111.1 us)
Async XLA Ops:
  7.2 42.5 %copy-start = (bf16[2,4,128,128]{3,2,1,0:T(8,128)(2,1)S(1)}, bf16[2,4,128,128]{3,2,1,0:T(8,128)(2,1)}, u32[]{:S(2)}) copy-start(bf16[2,4,128,128]{3,2,1,0:T(8,128)(2,1)} %param.14) | copy-start | bytes 786436
  12.9 25.3 %copy-start.1 = (bf16[256,512]{1,0:T(8,128)(2,1)S(1)}, bf16[256,512]{1,0:T(8,128)(2,1)}, u32[]{:S(2)}) copy-start(bf16[256,512]{1,0:T(8,128)(2,1)} %param.10) | copy-start | bytes 786436
  12.9 25.3 %copy-start.2 = (bf16[3,512,512]{2,1,0:T(8,128)(2,1)S(1)}, bf16[3,512,512]{2,1,0:T(8,128)(2,1)}, u32[]{:S(2)}) copy-start(bf16[3,512,512]{2,1,0:T(8,128)(2,1)} %param.12) | copy-start | bytes 4718596
  34.5 13.4 %all-to-all-start.1 = ((bf16[4,8,16,512]{3,2,0,1:T(8,128)(2,1)}), bf16[4,8,16,512]{3,2,0,1:T(8,128)(2,1)S(1)}, u32[]{:S(2)}, u32[]{:S(2)}) async-start(bf16[4,8,16,512]{3,2,0,1:T(8,128)(2,1)} %copy.193), calls=%async_computation.1 | async-start | bytes 1048576 | tf_op jit(solution)/shard_map/all_to_all | solution.py:56
  51.2 2.3 copy-start.10
  71.4 14.0 %all-to-all-start.3 = ((bf16[4,8,16,512]{3,2,0,1:T(8,128)(2,1)}), bf16[4,8,16,512]{3,2,0,1:T(8,128)(2,1)S(1)}, u32[]{:S(2)}, u32[]{:S(2)}) async-start(bf16[4,8,16,512]{3,2,0,1:T(8,128)(2,1)} %copy.195), calls=%async_computation.3 | async-start | bytes 1048576 | tf_op jit(solution)/shard_map/all_to_all | solution.py:56
  87.2 1.6 copy-start.17
  88.8 2.3 copy-start.11
  93.2 20.1 %copy-start.19 = (s32[2,4]{1,0:T(2,128)S(1)}, s32[2,4]{1,0:T(2,128)}, u32[]{:S(2)}) copy-start(s32[2,4]{1,0:T(2,128)} %param.15) | copy-start | bytes 100
  109.0 14.0 %all-to-all-start.5 = ((bf16[4,8,16,512]{3,2,0,1:T(8,128)(2,1)}), bf16[4,8,16,512]{3,2,0,1:T(8,128)(2,1)S(1)}, u32[]{:S(2)}, u32[]{:S(2)}) async-start(bf16[4,8,16,512]{3,2,0,1:T(8,128)(2,1)} %copy.197), calls=%async_computation.5 | async-start | bytes 1048576 | tf_op jit(solution)/shard_map/all_to_all | solution.py:56
  124.0 2.3 copy-start.13
  126.3 41.1 %copy-start.3 = (bf16[256,512]{1,0:T(8,128)(2,1)}, bf16[256,512]{1,0:T(8,128)(2,1)S(1)}, u32[]{:S(2)}) copy-start(bf16[256,512]{1,0:T(8,128)(2,1)S(1)} %multiply_convert_fusion.8) | copy-start | bytes 786436
  134.2 16.7 %all-to-all-start.6 = ((bf16[4,8,16,512]{3,2,1,0:T(8,128)(2,1)}), bf16[4,8,16,512]{3,2,1,0:T(8,128)(2,1)}, u32[]{:S(2)}, u32[]{:S(2)}) async-start(bf16[4,8,16,512]{3,2,1,0:T(8,128)(2,1)} %copy.203), calls=%async_computation.6 | async-start | bytes 1048576 | tf_op jit(solution)/shard_map/all_to_all | solution.py:101
  162.7 14.1 %all-to-all-start.7 = ((bf16[8,4,1,16,512]{4,3,1,2,0:T(8,128)(2,1)}), bf16[8,4,1,16,512]{4,3,1,2,0:T(8,128)(2,1)}, u32[]{:S(2)}, u32[]{:S(2)}) async-start(bf16[8,4,1,16,512]{4,3,1,2,0:T(8,128)(2,1)} %fusion.54), calls=%async_computation.7 | async-start | bytes 1048576 | tf_op jit(solution)/shard_map/all_to_all | solution.py:103
  178.3 4.0 copy-start.15
  190.3 16.7 %all-to-all-start.8 = ((bf16[4,8,16,512]{3,2,1,0:T(8,128)(2,1)}), bf16[4,8,16,512]{3,2,1,0:T(8,128)(2,1)}, u32[]{:S(2)}, u32[]{:S(2)}) async-start(bf16[4,8,16,512]{3,2,1,0:T(8,128)(2,1)} %copy.215), calls=%async_computation.8 | async-start | bytes 1048576 | tf_op jit(solution)/shard_map/all_to_all | solution.py:101
  194.5 2.4 copy-start.4
  196.9 1.7 copy-start.12
  218.7 14.0 %all-to-all-start.9 = ((bf16[8,4,1,16,512]{4,3,1,2,0:T(8,128)(2,1)}), bf16[8,4,1,16,512]{4,3,1,2,0:T(8,128)(2,1)S(1)}, u32[]{:S(2)}, u32[]{:S(2)}) async-start(bf16[8,4,1,16,512]{4,3,1,2,0:T(8,128)(2,1)} %fusion.46), calls=%async_computation.9 | async-start | bytes 1048576 | tf_op jit(solution)/shard_map/all_to_all | solution.py:103
  233.1 4.0 copy-start.14
  245.2 16.0 %all-to-all-start.10 = ((bf16[4,8,16,512]{3,2,1,0:T(8,128)(2,1)}), bf16[4,8,16,512]{3,2,1,0:T(8,128)(2,1)S(1)}, u32[]{:S(2)}, u32[]{:S(2)}) async-start(bf16[4,8,16,512]{3,2,1,0:T(8,128)(2,1)} %copy.232), calls=%async_computation.10 | async-start | bytes 1048576 | tf_op jit(solution)/shard_map/all_to_all | solution.py:101
  248.7 165.0 %all-reduce.3.cloned.1.call-start = ((), (), s32[]{:S(2)}) async-start(), calls=%async_computation.12 | async-start | bytes 12582912 | tf_op jit(solution)/shard_map/psum | solution.py:90
  266.1 17.6 %all-to-all-start.11 = ((bf16[8,4,1,16,512]{4,3,1,2,0:T(8,128)(2,1)}), bf16[8,4,1,16,512]{4,3,1,2,0:T(8,128)(2,1)S(1)}, u32[]{:S(2)}, u32[]{:S(2)}) async-start(bf16[8,4,1,16,512]{4,3,1,2,0:T(8,128)(2,1)} %fusion.38), calls=%async_computation.11 | async-start | bytes 1048576 | tf_op jit(solution)/shard_map/all_to_all | solution.py:103
  413.7 1.9 copy-start.8
  (7 other events, 9.6 us)
Sparse Core Ops, SparseCore 0:
  256.5 157.1 all-reduce.2
